TPU v7x, 32 devices: a whole 2x2x4 slice. The times are simulated.
32 devices in a mesh: row: 4 (over y, x), col: 8 (over z, core).
Axes of the slice: x: 2, y: 2, z: 4, core: 2. Of those that a mesh axis runs over, the one named last changes fastest.
Arguments:
- tiles: float32 [384, 1024, 128], P('row', 'col'), may hold values from -0.1875 to 0.1875
- tile_row: int32 [384, 8], P('row', 'col'), may hold values from 0 to 511
- tile_col: int32 [384, 8], P('row', 'col'), may hold values from 0 to 255
- tile_count: int32 [4, 8], P('row', 'col'), may hold values from 24 to 96, as said below
- cost: float32 [8, 32768], P('col', 'row'), may hold values from -6 to 6
- rhs: float32 [4, 65536], P('row', 'col'), may hold values from -6 to 6
- lower: float32 [8, 32768], P('col', 'row'), may hold values from -2 to -0.3
- upper: float32 [8, 32768], P('col', 'row'), may hold values from 0.3 to 2
- primal_start: float32 [8, 32768], P('col', 'row'), may hold values from -0.3 to 0.3
- dual_start: float32 [4, 65536], P('row', 'col'), may hold values from 0 to 1
Outputs:
- primal_mean: float32 [8, 32768], P('col', 'row')
- dual_mean: float32 [4, 65536], P('row', 'col')
- primal_last: float32 [8, 32768], P('col', 'row')
- dual_last: float32 [4, 65536], P('row', 'col')
Inputs may be any that keep to these rules, and one draw needn't show every extreme that they name: `tile_count`: live tiles of each device; some device holds 96.
All inputs are finite; a program needn't handle non-finite values.
Results may differ from a plain program's by a relative error of at most 0.0001.
Values sent between devices are 32-bit elements; how exact they have to be, the bound alone decides.
A program may use at most 64 MiB of HBM per device.

v0:
```python
import jax
import jax.numpy as jnp
from jax import lax
from jax.sharding import PartitionSpec as P

ITERS = 6


exact = lax.Precision.HIGHEST
primal_step = 0.3
dual_step = 0.3


def body(tiles, tile_row, tile_col, tile_count, cost, rhs, lower, upper, primal_start, dual_start):
    tile_slots = tiles.shape[0]
    block_size = tiles.shape[2]
    row_blocks = rhs.shape[1] * lax.axis_size("col") // block_size
    col_blocks = cost.shape[1] * lax.axis_size("row") // block_size
    live = (lax.iota(jnp.int32, tile_slots) < tile_count.reshape(())).astype(jnp.float32)
    row_hot = (tile_row[:, 0][:, None] == lax.iota(jnp.int32, row_blocks)[None, :]).astype(
        jnp.float32
    ) * live[:, None]
    col_hot = (tile_col[:, 0][:, None] == lax.iota(jnp.int32, col_blocks)[None, :]).astype(
        jnp.float32
    )
    primal = primal_start.reshape(-1)
    dual = dual_start.reshape(-1)
    cost_flat = cost.reshape(-1)
    lower_flat = lower.reshape(-1)
    upper_flat = upper.reshape(-1)
    rhs_flat = rhs.reshape(-1)
    primal_share = primal.shape[0]
    dual_share = dual.shape[0]
    primal_full, cost_full, lower_full, upper_full = (
        lax.all_gather(primal, "row", axis=0, tiled=True),
        lax.all_gather(cost_flat, "row", axis=0, tiled=True),
        lax.all_gather(lower_flat, "row", axis=0, tiled=True),
        lax.all_gather(upper_flat, "row", axis=0, tiled=True),
    )
    dual_full, rhs_full = (
        lax.all_gather(dual, "col", axis=0, tiled=True),
        lax.all_gather(rhs_flat, "col", axis=0, tiled=True),
    )
    extrapolated = primal_full
    primal_total = jnp.zeros_like(primal_full)
    dual_total = jnp.zeros_like(dual_full)
    for iteration in range(ITERS):
        forward_taken = jnp.dot(
            col_hot, extrapolated.reshape(col_blocks, block_size), precision=exact
        )
        forward_product = jnp.einsum("tij,tj->ti", tiles, forward_taken, precision=exact)
        applied = lax.psum(
            jnp.einsum("tr,ti->ri", row_hot, forward_product, precision=exact).reshape(-1), "col"
        )
        dual_full = jnp.maximum(dual_full + dual_step * (rhs_full - applied), 0.0)
        taken = jnp.dot(row_hot, dual_full.reshape(row_blocks, block_size), precision=exact)
        product = jnp.einsum("tij,ti->tj", tiles, taken, precision=exact)
        transposed = lax.psum(
            jnp.einsum("tk,tj->kj", col_hot, product, precision=exact).reshape(-1), "row"
        )
        moved = primal_full - primal_step * (cost_full - transposed)
        primal_new = jnp.minimum(jnp.maximum(moved, lower_full), upper_full)
        extrapolated = 2.0 * primal_new - primal_full
        primal_full = primal_new
        primal_total = primal_total + primal_full
        dual_total = dual_total + dual_full
    primal_start_at = lax.axis_index("row") * primal_share
    dual_start_at = lax.axis_index("col") * dual_share
    primal = lax.dynamic_slice_in_dim(primal_full, primal_start_at, primal_share, 0)
    dual = lax.dynamic_slice_in_dim(dual_full, dual_start_at, dual_share, 0)
    primal_mean = lax.dynamic_slice_in_dim(primal_total, primal_start_at, primal_share, 0) / ITERS
    dual_mean = lax.dynamic_slice_in_dim(dual_total, dual_start_at, dual_share, 0) / ITERS
    return (
        primal_mean.reshape(1, -1),
        dual_mean.reshape(1, -1),
        primal.reshape(1, -1),
        dual.reshape(1, -1),
    )


def solution(mesh):
    return jax.shard_map(
        body,
        mesh=mesh,
        in_specs=(
            P("row", "col", None),
            P("row", "col"),
            P("row", "col"),
            P("row", "col"),
            P("col", "row"),
            P("row", "col"),
            P("col", "row"),
            P("col", "row"),
            P("col", "row"),
            P("row", "col"),
        ),
        out_specs=(P("col", "row"), P("row", "col"), P("col", "row"), P("row", "col")),
        check_vma=False,
    )
```

profile of v0, /device:TPU:0, one launch (start us, length us, event | category | flops | bytes accessed | tf_op | source)
XLA Modules:
  0.0 754.1 jit_solution(14544451130449158460)
XLA Ops:
  7.2 10.1 %all-gather = f32[1,32768]{1,0:T(1,128)S(1)} all-gather(f32[1,8192]{1,0:T(1,128)} %param.18), channel_id=2, replica_groups=mesh['row'=4,'col'=8] {'row'}, dimensions={1}, use_global_device_ids=true | all-gather | bytes 163840 | tf_op jit(solution)/shard_map/all_gather | solution.py:35
  19.0 11.8 %fusion.119 = f32[96,1,128]{2,1,0:T(1,128)S(1)} fusion(f32[96,128,1]{1,2,0:T(1,128)S(1)} %bitcast.220, f32[96,128,128]{2,1,0:T(8,128)} %param.10), kind=kOutput, calls=%fused_computation.154 | convolution fusion | flops 18874368 | bytes 6389760 | tf_op jit(solution)/shard_map/tij,tj->ti/dot_general | solution.py:51
  30.8 1.4 convolution_bitcast_fusion.5
  32.3 14.5 %all-gather.3 = f32[1,65536]{1,0:T(1,128)S(1)} all-gather(f32[1,8192]{1,0:T(1,128)S(1)} %copy-done.2), channel_id=5, replica_groups=mesh['row'=4,'col'=8] {'col'}, dimensions={1}, use_global_device_ids=true | all-gather | bytes 294912 | tf_op jit(solution)/shard_map/all_gather | solution.py:42
  46.8 14.3 %all-gather.2 = f32[1,65536]{1,0:T(1,128)S(1)} all-gather(f32[1,8192]{1,0:T(1,128)S(1)} %copy-done.3), channel_id=4, replica_groups=mesh['row'=4,'col'=8] {'col'}, dimensions={1}, use_global_device_ids=true | all-gather | bytes 294912 | tf_op jit(solution)/shard_map/all_gather | solution.py:41
  61.1 27.2 %all-reduce.13.cloned.1.call-done = f32[65536]{0:T(1024)} async-done(((f32[65536]{0:T(1024)}), f32[65536]{0:T(1024)}) %all-reduce.13.cloned.1.call-update) | async-done | bytes 262160 | tf_op jit(solution)/shard_map/psum | solution.py:52
  88.3 1.0 add_maximum_fusion.5
  89.7 7.3 fusion.120
  97.0 1.0 convolution_bitcast_fusion.11
  98.2 8.4 %all-gather.1 = f32[1,32768]{1,0:T(1,128)S(1)} all-gather(f32[1,8192]{1,0:T(1,128)S(1)} %copy-done.4), channel_id=3, replica_groups=mesh['row'=4,'col'=8] {'row'}, dimensions={1}, use_global_device_ids=true | all-gather | bytes 163840 | tf_op jit(solution)/shard_map/all_gather | solution.py:36
  106.6 8.8 %all-gather.4 = f32[1,32768]{1,0:T(1,128)S(1)} all-gather(f32[1,8192]{1,0:T(1,128)S(1)} %copy-done.5), channel_id=6, replica_groups=mesh['row'=4,'col'=8] {'row'}, dimensions={1}, use_global_device_ids=true | all-gather | bytes 163840 | tf_op jit(solution)/shard_map/all_gather | solution.py:37
  115.4 7.3 all-gather.5
  122.7 16.8 %all-reduce.15.cloned.1.call-done = f32[32768]{0:T(1024)} async-done(((f32[32768]{0:T(1024)}), f32[32768]{0:T(1024)}) %all-reduce.15.cloned.1.call-update) | async-done | bytes 131088 | tf_op jit(solution)/shard_map/psum | solution.py:58
  140.7 11.8 %fusion.121 = f32[96,1,128]{2,1,0:T(1,128)S(1)} fusion(f32[96,128,1]{1,2,0:T(1,128)S(1)} %bitcast.198, f32[96,128,128]{2,1,0:T(8,128)} %param.10), kind=kOutput, calls=%fused_computation.156 | convolution fusion | flops 18874368 | bytes 6389760 | tf_op jit(solution)/shard_map/tij,tj->ti/dot_general | solution.py:51
  152.5 1.4 convolution_bitcast_fusion.4
  154.0 55.5 %all-reduce.17.cloned.1.call-done = f32[65536]{0:T(1024)} async-done(((f32[65536]{0:T(1024)}), f32[65536]{0:T(1024)}) %all-reduce.17.cloned.1.call-update) | async-done | bytes 262160 | tf_op jit(solution)/shard_map/psum | solution.py:52
  209.5 1.0 add_maximum_fusion.4
  210.9 7.3 fusion.122
  218.2 1.0 convolution_bitcast_fusion.10
  219.7 41.0 %all-reduce.19.cloned.1.call-done = f32[32768]{0:T(1024)} async-done(((f32[32768]{0:T(1024)}), f32[32768]{0:T(1024)}) %all-reduce.19.cloned.1.call-update) | async-done | bytes 131088 | tf_op jit(solution)/shard_map/psum | solution.py:58
  261.9 11.8 %fusion.123 = f32[96,1,128]{2,1,0:T(1,128)S(1)} fusion(f32[96,128,1]{1,2,0:T(1,128)S(1)} %bitcast.207, f32[96,128,128]{2,1,0:T(8,128)} %param.10), kind=kOutput, calls=%fused_computation.158 | convolution fusion | flops 18874368 | bytes 6389760 | tf_op jit(solution)/shard_map/tij,tj->ti/dot_general | solution.py:51
  273.7 1.4 convolution_bitcast_fusion.3
  275.2 55.5 %all-reduce.21.cloned.1.call-done = f32[65536]{0:T(1024)} async-done(((f32[65536]{0:T(1024)}), f32[65536]{0:T(1024)}) %all-reduce.21.cloned.1.call-update) | async-done | bytes 262160 | tf_op jit(solution)/shard_map/psum | solution.py:52
  330.7 1.0 add_maximum_fusion.3
  332.1 7.3 fusion.124
  339.4 1.0 convolution_bitcast_fusion.9
  340.5 41.4 %all-reduce.23.cloned.1.call-done = f32[32768]{0:T(1024)} async-done(((f32[32768]{0:T(1024)}), f32[32768]{0:T(1024)}) %all-reduce.23.cloned.1.call-update) | async-done | bytes 131088 | tf_op jit(solution)/shard_map/psum | solution.py:58
  383.1 11.8 %fusion.125 = f32[96,1,128]{2,1,0:T(1,128)S(1)} fusion(f32[96,128,1]{1,2,0:T(1,128)S(1)} %bitcast.209, f32[96,128,128]{2,1,0:T(8,128)} %param.10), kind=kOutput, calls=%fused_computation.160 | convolution fusion | flops 18874368 | bytes 6389760 | tf_op jit(solution)/shard_map/tij,tj->ti/dot_general | solution.py:51
  394.9 1.4 convolution_bitcast_fusion.2
  396.5 55.3 %all-reduce.25.cloned.1.call-done = f32[65536]{0:T(1024)} async-done(((f32[65536]{0:T(1024)}), f32[65536]{0:T(1024)}) %all-reduce.25.cloned.1.call-update) | async-done | bytes 262160 | tf_op jit(solution)/shard_map/psum | solution.py:52
  451.9 1.0 add_maximum_fusion.2
  453.3 7.3 fusion.126
  460.6 1.0 convolution_bitcast_fusion.8
  461.7 41.4 %all-reduce.27.cloned.1.call-done = f32[32768]{0:T(1024)} async-done(((f32[32768]{0:T(1024)}), f32[32768]{0:T(1024)}) %all-reduce.27.cloned.1.call-update) | async-done | bytes 131088 | tf_op jit(solution)/shard_map/psum | solution.py:58
  504.2 11.8 %fusion.127 = f32[96,1,128]{2,1,0:T(1,128)S(1)} fusion(f32[96,128,1]{1,2,0:T(1,128)S(1)} %bitcast.211, f32[96,128,128]{2,1,0:T(8,128)} %param.10), kind=kOutput, calls=%fused_computation.162 | convolution fusion | flops 18874368 | bytes 6389760 | tf_op jit(solution)/shard_map/tij,tj->ti/dot_general | solution.py:51
  516.1 1.4 convolution_bitcast_fusion.1
  517.5 55.5 %all-reduce.29.cloned.1.call-done = f32[65536]{0:T(1024)} async-done(((f32[65536]{0:T(1024)}), f32[65536]{0:T(1024)}) %all-reduce.29.cloned.1.call-update) | async-done | bytes 262160 | tf_op jit(solution)/shard_map/psum | solution.py:52
  573.1 1.0 add_maximum_fusion.1
  574.4 7.3 fusion.128
  581.8 1.0 convolution_bitcast_fusion.7
  583.1 41.2 %all-reduce.31.cloned.1.call-done = f32[32768]{0:T(1024)} async-done(((f32[32768]{0:T(1024)}), f32[32768]{0:T(1024)}) %all-reduce.31.cloned.1.call-update) | async-done | bytes 131088 | tf_op jit(solution)/shard_map/psum | solution.py:58
  625.4 11.8 %fusion.129 = f32[96,1,128]{2,1,0:T(1,128)S(1)} fusion(f32[96,128,1]{1,2,0:T(1,128)S(1)} %bitcast.213, f32[96,128,128]{2,1,0:T(8,128)} %param.10), kind=kOutput, calls=%fused_computation.164 | convolution fusion | flops 18874368 | bytes 6389760 | tf_op jit(solution)/shard_map/tij,tj->ti/dot_general | solution.py:51
  637.3 1.4 convolution_bitcast_fusion
  638.7 55.5 %all-reduce.33.cloned.1.call-done = f32[65536]{0:T(1024)} async-done(((f32[65536]{0:T(1024)}), f32[65536]{0:T(1024)}) %all-reduce.33.cloned.1.call-update) | async-done | bytes 262160 | tf_op jit(solution)/shard_map/psum | solution.py:52
  694.2 1.0 add_maximum_fusion
  695.6 7.3 fusion.130
  702.9 1.0 convolution_bitcast_fusion.6
  704.6 40.8 %all-reduce.35.cloned.1.call-done = f32[32768]{0:T(1024)} async-done(((f32[32768]{0:T(1024)}), f32[32768]{0:T(1024)}) %all-reduce.35.cloned.1.call-update) | async-done | bytes 131088 | tf_op jit(solution)/shard_map/psum | solution.py:58
  (59 shorter events, 12.8 us)
Async XLA Ops:
  7.2 23.7 %copy-start = (s32[96,1]{0,1:T(1,128)S(1)}, s32[96,1]{0,1:T(1,128)}, u32[]{:S(2)}) copy-start(s32[96,1]{0,1:T(1,128)} %param.11) | copy-start | bytes 1156
  7.2 25.1 %copy-start.2 = (f32[1,8192]{1,0:T(1,128)S(1)}, f32[1,8192]{1,0:T(1,128)}, u32[]{:S(2)}) copy-start(f32[1,8192]{1,0:T(1,128)} %param.15) | copy-start | bytes 98308
  7.2 39.6 %copy-start.3 = (f32[1,8192]{1,0:T(1,128)S(1)}, f32[1,8192]{1,0:T(1,128)}, u32[]{:S(2)}) copy-start(f32[1,8192]{1,0:T(1,128)} %param.19) | copy-start | bytes 98308
  7.2 81.1 %all-reduce.13.cloned.1.call-start = ((), (), s32[]{:S(2)}) async-start(), calls=%async_computation | async-start | bytes 524288 | tf_op jit(solution)/shard_map/psum | solution.py:52
  18.9 78.1 %copy-start.1 = (s32[96,1]{0,1:T(1,128)S(1)}, s32[96,1]{0,1:T(1,128)}, u32[]{:S(2)}) copy-start(s32[96,1]{0,1:T(1,128)} %param.12) | copy-start | bytes 1156
  19.0 79.2 %copy-start.4 = (f32[1,8192]{1,0:T(1,128)S(1)}, f32[1,8192]{1,0:T(1,128)}, u32[]{:S(2)}) copy-start(f32[1,8192]{1,0:T(1,128)} %param.14) | copy-start | bytes 98308
  30.8 75.8 %copy-start.5 = (f32[1,8192]{1,0:T(1,128)S(1)}, f32[1,8192]{1,0:T(1,128)}, u32[]{:S(2)}) copy-start(f32[1,8192]{1,0:T(1,128)} %param.16) | copy-start | bytes 98308
  30.8 84.6 %copy-start.6 = (f32[1,8192]{1,0:T(1,128)S(1)}, f32[1,8192]{1,0:T(1,128)}, u32[]{:S(2)}) copy-start(f32[1,8192]{1,0:T(1,128)} %param.17) | copy-start | bytes 98308
  32.2 107.3 %all-reduce.15.cloned.1.call-start = ((), (), s32[]{:S(2)}) async-start(), calls=%async_computation.1 | async-start | bytes 262144 | tf_op jit(solution)/shard_map/psum | solution.py:58
  98.1 111.4 %all-reduce.17.cloned.1.call-start = ((), (), s32[]{:S(2)}) async-start(), calls=%async_computation.2 | async-start | bytes 524288 | tf_op jit(solution)/shard_map/psum | solution.py:52
  154.0 106.7 %all-reduce.19.cloned.1.call-start = ((), (), s32[]{:S(2)}) async-start(), calls=%async_computation.3 | async-start | bytes 262144 | tf_op jit(solution)/shard_map/psum | solution.py:58
  219.3 111.4 %all-reduce.21.cloned.1.call-start = ((), (), s32[]{:S(2)}) async-start(), calls=%async_computation.4 | async-start | bytes 524288 | tf_op jit(solution)/shard_map/psum | solution.py:52
  275.1 106.7 %all-reduce.23.cloned.1.call-start = ((), (), s32[]{:S(2)}) async-start(), calls=%async_computation.5 | async-start | bytes 262144 | tf_op jit(solution)/shard_map/psum | solution.py:58
  340.5 111.4 %all-reduce.25.cloned.1.call-start = ((), (), s32[]{:S(2)}) async-start(), calls=%async_computation.6 | async-start | bytes 524288 | tf_op jit(solution)/shard_map/psum | solution.py:52
  396.3 106.7 %all-reduce.27.cloned.1.call-start = ((), (), s32[]{:S(2)}) async-start(), calls=%async_computation.7 | async-start | bytes 262144 | tf_op jit(solution)/shard_map/psum | solution.py:58
  461.6 111.4 %all-reduce.29.cloned.1.call-start = ((), (), s32[]{:S(2)}) async-start(), calls=%async_computation.8 | async-start | bytes 524288 | tf_op jit(solution)/shard_map/psum | solution.py:52
  517.5 106.7 %all-reduce.31.cloned.1.call-start = ((), (), s32[]{:S(2)}) async-start(), calls=%async_computation.9 | async-start | bytes 262144 | tf_op jit(solution)/shard_map/psum | solution.py:58
  582.8 111.4 %all-reduce.33.cloned.1.call-start = ((), (), s32[]{:S(2)}) async-start(), calls=%async_computation.10 | async-start | bytes 524288 | tf_op jit(solution)/shard_map/psum | solution.py:52
  638.7 106.7 %all-reduce.35.cloned.1.call-start = ((), (), s32[]{:S(2)}) async-start(), calls=%async_computation.11 | async-start | bytes 262144 | tf_op jit(solution)/shard_map/psum | solution.py:58
Sparse Core Ops, SparseCore 0:
  32.4 55.9 all-reduce.12
  98.2 41.2 all-reduce.14
  154.1 55.4 all-reduce.16
  219.4 41.2 all-reduce.18
  275.3 55.4 all-reduce.20
  340.6 41.2 all-reduce.22
  396.4 55.4 all-reduce.24
  461.8 41.2 all-reduce.26
  517.6 55.4 all-reduce.28
  582.9 41.2 all-reduce.30
  638.8 55.4 all-reduce.32
  704.1 41.2 all-reduce.34
where the time goes:
time: 762 us; the launch traced here: 754 us
  waiting for transfers between devices  527 us (69%)
  matrix products  134 us (18%)
  blocking collectives  63.5 us (8%)
  between operations  15.3 us (2%)
  other arithmetic  12.9 us (2%)
    psum x6, waiting for transfers between devices, body(): lax.psum(jnp.einsum('tr,ti->ri', row_hot, forward_product, precision=exac...  305 us
    psum x6, waiting for transfers between devices, body(): lax.psum(jnp.einsum('tk,tj->kj', col_hot, product, precision=exact).resha...  222 us
    dot_general x6, matrix products, body(): jnp.einsum('tij,tj->ti', tiles, forward_taken, precision=exact)  71.1 us
    dot_general x6, matrix products, body(): product = jnp.einsum('tij,ti->tj', tiles, taken, precision=exact)  43.9 us
  transfers between devices with their start and end apart: 12, of which 12 were waited for; matrix products, arithmetic and copies ran while one was open for 0% of the time, Pallas kernels for 0%

commit v1 on v0

v1 whole, which is shorter than its diff:
```python
import functools

import jax
import jax.numpy as jnp
from jax import lax
from jax.experimental import pallas as pl
from jax.experimental.pallas import tpu as pltpu
from jax.sharding import PartitionSpec as P

ITERS = 6
primal_step = 0.3
dual_step = 0.3
SUB = 8


def split_dot(hot, data):
    high = data.astype(jnp.bfloat16)
    rest = data - high.astype(jnp.float32)
    middle = rest.astype(jnp.bfloat16)
    low = (rest - middle.astype(jnp.float32)).astype(jnp.bfloat16)
    dot = functools.partial(jnp.dot, preferred_element_type=jnp.float32)
    return (dot(hot, low) + dot(hot, middle)) + dot(hot, high)


def kernel(
    n_row, n_col,
    tiles_hbm, tile_row, tile_col, tile_count, cost, rhs, lower, upper, primal_start, dual_start,
    primal_mean, dual_mean, primal_last, dual_last,
    tiles, flipped, y_init, x_init, c_init, z_all, p_all, y_hot, x_hot, y_column, x_column,
    y_state, b_state, x_state, c_state, l_state, u_state, extrapolated, y_total, x_total,
    tile_sem, z_send, z_recv, p_send, p_recv, yi_send, yi_recv, xi_send, xi_recv, ci_send, ci_recv,
):
    slots = tile_row.shape[0]
    sy = rhs.shape[0]
    sx = cost.shape[0]
    row = lax.axis_index("row")
    col = lax.axis_index("col")
    chips = n_col // 2
    chip = col // 2
    core = col % 2
    partner = chip * 2 + (1 - core)

    def chip_to(d):
        return ((chip + d) % chips) * 2 + core

    def chip_from(d):
        return ((chip + chips - d) % chips) * 2 + core

    def row_to(d):
        return (row + d) % n_row

    def row_from(d):
        return (row + n_row - d) % n_row

    tile_copy = pltpu.make_async_copy(tiles_hbm, tiles, tile_sem)
    tile_copy.start()

    barrier = pltpu.get_barrier_semaphore()
    for d in range(1, n_row):
        pl.semaphore_signal(barrier, inc=1, device_id={"row": row_to(d)}, device_id_type=pl.DeviceIdType.MESH)
    for d in range(1, chips):
        pl.semaphore_signal(barrier, inc=1, device_id={"col": chip_to(d)}, device_id_type=pl.DeviceIdType.MESH)
    pl.semaphore_signal(barrier, inc=1, device_id={"col": partner}, device_id_type=pl.DeviceIdType.MESH)

    live = lax.broadcasted_iota(jnp.int32, (slots, 1), 0) < tile_count[...]
    row_ids = tile_row[...].astype(jnp.float32)
    col_ids = tile_col[...].astype(jnp.float32)

    def as_row(ids):
        wide = jnp.broadcast_to(jnp.where(live, ids, -1.0), (slots, 128))
        if slots < 128:
            wide = jnp.concatenate([wide, jnp.full((128 - slots, 128), -1.0, jnp.float32)], axis=0)
        return wide.T[:SUB, :]

    x_init[row, 0:sx, :] = primal_start[...]
    x_init[row, sx : sx + SUB, :] = as_row(col_ids)
    y_init[col, 0:sy, :] = dual_start[...]
    y_init[col, sy : 2 * sy, :] = rhs[...]
    y_init[col, 2 * sy : 2 * sy + SUB, :] = as_row(row_ids)
    c_init[row, 0:sx, :] = cost[...]
    c_init[row, sx : 2 * sx, :] = lower[...]
    c_init[row, 2 * sx : 3 * sx, :] = upper[...]

    pl.semaphore_wait(barrier, (n_row - 1) + (chips - 1) + 1)

    def remote(place, send, recv, target):
        return pltpu.make_async_remote_copy(
            src_ref=place, dst_ref=place, send_sem=send, recv_sem=recv,
            device_id=target, device_id_type=pl.DeviceIdType.MESH,
        )

    def row_send(place_of, send, recv):
        for d in range(1, n_row):
            remote(place_of(row), send(d - 1), recv(d - 1), {"row": row_to(d)}).start()

    def row_wait(place_of, send, recv):
        for d in range(1, n_row):
            remote(place_of(row_from(d)), send(d - 1), recv(d - 1), {"row": row_to(d)}).wait_recv()
        for d in range(1, n_row):
            remote(place_of(row), send(d - 1), recv(d - 1), {"row": row_to(d)}).wait_send()

    near_first = sorted(range(1, chips), key=lambda d: min(d, chips - d))

    def col_send(place_of, send, recv):
        for d in near_first:
            remote(place_of(col), send(d - 1), recv(d - 1), {"col": chip_to(d)}).start()
        remote(place_of(col), send(chips - 1), recv(chips - 1), {"col": partner}).start()

    def other(index):
        return index + 1 - 2 * core

    def col_wait(place_of, send, recv):
        for d in near_first:
            remote(place_of(chip_from(d)), send(d - 1), recv(d - 1), {"col": chip_to(d)}).wait_recv()
            remote(place_of(chip_from(d)), send(chips + d - 1), recv(chips + d - 1), {"col": partner}).start()
        remote(place_of(partner), send(chips - 1), recv(chips - 1), {"col": partner}).wait_recv()
        for d in near_first:
            remote(
                place_of(other(chip_from(d))), send(chips + d - 1), recv(chips + d - 1), {"col": partner}
            ).wait_recv()
        for d in near_first:
            remote(place_of(col), send(d - 1), recv(d - 1), {"col": chip_to(d)}).wait_send()
            remote(place_of(chip_from(d)), send(chips + d - 1), recv(chips + d - 1), {"col": partner}).wait_send()
        remote(place_of(col), send(chips - 1), recv(chips - 1), {"col": partner}).wait_send()

    xi = (lambda i: x_init.at[i], lambda k: xi_send.at[k], lambda k: xi_recv.at[k])
    ci = (lambda i: c_init.at[i], lambda k: ci_send.at[k], lambda k: ci_recv.at[k])
    yi = (lambda i: y_init.at[i], lambda k: yi_send.at[k], lambda k: yi_recv.at[k])
    row_send(*xi)
    col_send(*yi)
    row_send(*ci)

    tile_copy.wait()

    def flip(t, carry):
        flipped[t] = tiles[t].T
        return carry

    lax.fori_loop(0, slots, flip, 0, unroll=4)

    def hot_of(ids, first, share, column, hot, init, at, n):
        for i in range(n):
            block = init[i, at : at + SUB, :].T
            column[i * slots : (i + 1) * slots, :] = jnp.broadcast_to(block[:slots, 0:1], (slots, 128))
        wide = column[...].T[0:1, :]
        own = first + lax.broadcasted_iota(jnp.int32, (share, 1), 0)
        hot[0:slots, :] = jnp.where(ids == wide, 1.0, 0.0).astype(jnp.bfloat16)
        hot[slots : slots + share, :] = jnp.where(own.astype(jnp.float32) == wide, 1.0, 0.0).astype(jnp.bfloat16)

    def pick_of(ids, blocks):
        return jnp.where(
            ids == lax.broadcasted_iota(jnp.int32, (slots, blocks), 1), 1.0, 0.0
        ).astype(jnp.bfloat16)

    def place_state(state, pick, init, at, share, own, n):
        whole = init[:, at : at + share, :].reshape(n * share, 128)
        state[0:slots, :] = split_dot(pick, whole)
        state[slots : slots + share, :] = own[...]

    row_wait(*xi)
    x_pick = pick_of(tile_col[...], n_row * sx)
    place_state(x_state, x_pick, x_init, 0, sx, primal_start, n_row)
    extrapolated[...] = x_state[0:slots, :]
    hot_of(col_ids, row * sx, sx, x_column, x_hot, x_init, sx, n_row)

    col_wait(*yi)
    y_pick = pick_of(tile_row[...], n_col * sy)
    place_state(y_state, y_pick, y_init, 0, sy, dual_start, n_col)
    place_state(b_state, y_pick, y_init, sy, sy, rhs, n_col)
    hot_of(row_ids, col * sy, sy, y_column, y_hot, y_init, 2 * sy, n_col)

    row_wait(*ci)
    place_state(c_state, x_pick, c_init, 0, sx, cost, n_row)
    place_state(l_state, x_pick, c_init, sx, sx, lower, n_row)
    place_state(u_state, x_pick, c_init, 2 * sx, sx, upper, n_row)

    y_total[...] = jnp.zeros_like(y_total)
    x_total[...] = jnp.zeros_like(x_total)

    def products(blocks, vectors, out):
        def group(g, carry):
            at = pl.multiple_of(g * SUB, SUB)
            columns = vectors[pl.ds(at, SUB), :].T
            rows = [
                jnp.sum(blocks[at + k] * columns[:, k : k + 1], axis=0, keepdims=True) for k in range(SUB)
            ]
            out[pl.ds(at, SUB), :] = jnp.concatenate(rows, axis=0)
            return carry

        lax.fori_loop(0, slots // SUB, group, 0, unroll=2)

    def iteration(step, carry):
        now = step % 2
        z = (lambda i: z_all.at[now, i], lambda k: z_send.at[now, k], lambda k: z_recv.at[now, k])
        p = (lambda i: p_all.at[now, i], lambda k: p_send.at[now, k], lambda k: p_recv.at[now, k])
        products(flipped, extrapolated, z_all.at[now, col])
        col_send(*z)
        col_wait(*z)
        applied = split_dot(y_hot[...], z_all[now].reshape(n_col * slots, 128))
        y_new = jnp.maximum(y_state[...] + dual_step * (b_state[...] - applied), 0.0)
        y_state[...] = y_new
        y_total[...] += y_new[slots:, :]
        products(tiles, y_state, p_all.at[now, row])
        row_send(*p)
        row_wait(*p)
        transposed = split_dot(x_hot[...], p_all[now].reshape(n_row * slots, 128))
        x_old = x_state[...]
        moved = x_old - primal_step * (c_state[...] - transposed)
        x_new = jnp.minimum(jnp.maximum(moved, l_state[...]), u_state[...])
        x_state[...] = x_new
        extrapolated[...] = 2.0 * x_new[:slots, :] - x_old[:slots, :]
        x_total[...] += x_new[slots:, :]
        return carry

    lax.fori_loop(0, ITERS, iteration, 0)

    primal_last[...] = x_state[slots:, :]
    dual_last[...] = y_state[slots:, :]
    primal_mean[...] = x_total[...] / ITERS
    dual_mean[...] = y_total[...] / ITERS


def body(n_row, n_col, tiles, tile_row, tile_col, tile_count, cost, rhs, lower, upper, primal_start, dual_start):
    slots, bs = tiles.shape[0], tiles.shape[2]
    blocks = [a.reshape(-1, bs) for a in (cost, rhs, lower, upper, primal_start, dual_start)]
    sx, sy = blocks[0].shape[0], blocks[1].shape[0]
    f32 = jnp.float32
    chips = n_col // 2
    vmem = pl.BlockSpec(memory_space=pltpu.VMEM)
    dma = pltpu.SemaphoreType.DMA
    state = lambda share: pltpu.VMEM((slots + share, bs), f32)
    out = pl.pallas_call(
        functools.partial(kernel, n_row, n_col),
        out_shape=[jax.ShapeDtypeStruct((s, bs), f32) for s in (sx, sy, sx, sy)],
        in_specs=[pl.BlockSpec(memory_space=pl.ANY)] + [vmem] * 9,
        out_specs=[vmem] * 4,
        scratch_shapes=[
            pltpu.VMEM(tiles.shape, f32),
            pltpu.VMEM(tiles.shape, f32),
            pltpu.VMEM((n_col, 2 * sy + SUB, bs), f32),
            pltpu.VMEM((n_row, sx + SUB, bs), f32),
            pltpu.VMEM((n_row, 3 * sx, bs), f32),
            pltpu.VMEM((2, n_col, slots, bs), f32),
            pltpu.VMEM((2, n_row, slots, bs), f32),
            pltpu.VMEM((slots + sy, n_col * slots), jnp.bfloat16),
            pltpu.VMEM((slots + sx, n_row * slots), jnp.bfloat16),
            pltpu.VMEM((n_col * slots, bs), f32),
            pltpu.VMEM((n_row * slots, bs), f32),
            state(sy), state(sy), state(sx), state(sx), state(sx), state(sx),
            pltpu.VMEM((slots, bs), f32),
            pltpu.VMEM((sy, bs), f32),
            pltpu.VMEM((sx, bs), f32),
            dma,
            dma((2, 2 * chips)), dma((2, 2 * chips)),
            dma((2, n_row)), dma((2, n_row)),
            dma((2 * chips,)), dma((2 * chips,)),
            dma((n_row,)), dma((n_row,)),
            dma((n_row,)), dma((n_row,)),
        ],
        compiler_params=pltpu.CompilerParams(
            collective_id=0, has_side_effects=True, vmem_limit_bytes=40 * 1024 * 1024
        ),
        name="pdhg",
    )(tiles, tile_row, tile_col, tile_count, *blocks)
    return tuple(a.reshape(1, -1) for a in out)


def solution(mesh):
    return jax.shard_map(
        functools.partial(body, mesh.shape["row"], mesh.shape["col"]),
        mesh=mesh,
        in_specs=(
            P("row", "col", None),
            P("row", "col"),
            P("row", "col"),
            P("row", "col"),
            P("col", "row"),
            P("row", "col"),
            P("col", "row"),
            P("col", "row"),
            P("col", "row"),
            P("row", "col"),
        ),
        out_specs=(P("col", "row"), P("row", "col"), P("col", "row"), P("row", "col")),
        check_vma=False,
    )
```

time: 762 us -> 132 us (0.17)
  waiting for transfers between devices: 527 us -> 0 us
  matrix products: 134 us -> 0 us
  Pallas kernels: 0 us -> 119 us
  blocking collectives: 63.5 us -> 0 us
  between operations: 15.3 us -> 1.3 us
  other arithmetic: 12.9 us -> 0 us
  local copies, waits for them, and re-layouts: 0.04 us -> 11.3 us
    psum x12 -> x0, waiting for transfers between devices: 527 us -> none  [the longest x6 305 us: body(): lax.psum(jnp.einsum('tr,ti->ri', row_hot, forward_product, precision=exac...]
    dot_general x36 -> x0, matrix products: 134 us -> none  [the longest x6 71.1 us: body(): jnp.einsum('tij,tj->ti', tiles, forward_taken, precision=exact)]
    pallas_call x0 -> x1, Pallas kernels: none -> 119 us  [body(): pl.pallas_call(functools.partial(kernel, n_row, n_col), out_shape=[jax.Sh...]
    all_gather x6 -> x0, blocking collectives: 63.5 us -> none  [the longest x1 14.5 us: body(): lax.all_gather(rhs_flat, 'col', axis=0, tiled=True)]
    unnamed x14 -> x20, local copies, waits for them, and re-layouts: 0.04 us -> 11.3 us
  transfers between devices with their start and end apart: 12 -> 0, of which waited for: 12 -> 0; matrix products, arithmetic and copies ran while one was open for 0% -> 0% of each run, Pallas kernels for 0% -> 0%
where the time goes in v1:
time: 132 us; the launch traced here: 131 us
  Pallas kernels  119 us (90%)
  local copies, waits for them, and re-layouts  11.3 us (9%)
    pallas_call x1, Pallas kernels, body(): pl.pallas_call(functools.partial(kernel, n_row, n_col), out_shape=[jax.Sh...  119 us
    unnamed x20, local copies, waits for them, and re-layouts  11.3 us

profile of v1, /device:TPU:0, one launch (start us, length us, event | category | flops | bytes accessed | tf_op | source)
XLA Modules:
  0.0 131.4 jit_solution(7201632209341743918)
XLA Ops:
  1.3 0.8 copy.14.tile_row
  2.0 0.8 copy.15.tile_col
  2.8 0.0 copy-start
  2.8 2.8 %copy-done = f32[96,128,128]{2,1,0:T(8,128)S(1)} copy-done((f32[96,128,128]{2,1,0:T(8,128)S(1)}, f32[96,128,128]{2,1,0:T(8,128)}, u32[]{:S(2)}) %copy-start) | copy-done | bytes 6291480
  5.6 0.0 copy-start.1
  5.6 0.8 copy-done.1
  6.3 0.0 copy-start.2
  6.3 0.8 copy-done.2
  7.1 0.0 copy-start.3
  7.1 0.8 copy-done.3
  7.8 0.0 copy-start.4
  7.8 0.8 copy-done.4
  8.6 0.0 copy-start.5
  8.6 0.8 copy-done.5
  9.4 0.0 copy-start.6
  9.4 0.8 copy-done.6
  10.1 118.8 %pdhg.1 = (f32[64,128]{1,0:T(8,128)S(1)}, f32[64,128]{1,0:T(8,128)S(1)}, f32[64,128]{1,0:T(8,128)S(1)}, f32[64,128]{1,0:T(8,128)S(1)}) custom-call(f32[96,128,128]{2,1,0:T(8,128)S(1)} %copy-done, s32[96,1]{1,0:T(8,128)S(1)} %copy.14.tile_row, s32[96,1]{1,0:T(8,128)S(1)} %copy.15.tile_col, s32[1,1]{1,0:T(1,128)S(6)} %copy.20.tile_count, ...), custom_call_target="tpu_custom_call" | custom-call | tf_op jit(solution)/shard_map/pdhg/pallas_call | solution.py:232
  129.0 0.6 copy.21
  129.6 0.6 copy.22
  130.2 0.6 copy.23
  130.8 0.6 copy.24
Async XLA Ops:
  2.8 2.8 %copy-start = (f32[96,128,128]{2,1,0:T(8,128)S(1)}, f32[96,128,128]{2,1,0:T(8,128)}, u32[]{:S(2)}) copy-start(f32[96,128,128]{2,1,0:T(8,128)} %tiles_hbm.1) | copy-start | bytes 18874372
  5.6 0.8 copy-start.1
  6.3 0.8 copy-start.2
  7.1 0.8 copy-start.3
  7.8 0.8 copy-start.4
  8.6 0.8 copy-start.5
  9.4 0.8 copy-start.6

commit v2 on v1

v2 whole, which is shorter than its diff:
```python
import functools

import jax
import jax.numpy as jnp
from jax import lax
from jax.experimental import pallas as pl
from jax.experimental.pallas import tpu as pltpu
from jax.sharding import PartitionSpec as P

ITERS = 6
primal_step = 0.3
dual_step = 0.3
SUB = 8
CHUNKS = 2
TILE_PARTS = 4
UNROLL = 6


def split_dot(hot, data):
    high = data.astype(jnp.bfloat16)
    rest = data - high.astype(jnp.float32)
    middle = rest.astype(jnp.bfloat16)
    low = (rest - middle.astype(jnp.float32)).astype(jnp.bfloat16)
    dot = functools.partial(jnp.dot, preferred_element_type=jnp.float32)
    return (dot(hot, low) + dot(hot, middle)) + dot(hot, high)


def pieces_of(data):
    high = data.astype(jnp.bfloat16).astype(jnp.float32)
    rest = data - high
    middle = rest.astype(jnp.bfloat16).astype(jnp.float32)
    return high, middle, rest - middle


def kernel(
    n_row, n_col,
    tiles_hbm, tile_row, tile_col, tile_count, cost, rhs, lower, upper, primal_start, dual_start,
    primal_mean, dual_mean, primal_last, dual_last,
    tiles, plain, flipped, y_init, x_init, c_init, z_all, p_all, y_hot, x_hot, y_column, x_column,
    y_state, b_state, x_state, c_state, l_state, u_state, extrapolated, y_total, x_total,
    tile_sem, in_sem, z_send, z_recv, p_send, p_recv, yi_send, yi_recv, xi_send, xi_recv, ci_send, ci_recv,
):
    slots = tile_row.shape[1]
    sy = rhs.shape[0]
    sx = cost.shape[0]
    row = lax.axis_index("row")
    col = lax.axis_index("col")
    chips = n_col // 2
    chip = col // 2
    core = col % 2
    partner = chip * 2 + (1 - core)
    high_half = (chip * 2) // chips

    def chip_at(k):
        down = chips - 1 - k
        down = down - (chip - down + chips) // chips
        up = k + (k - chip + chips) // chips
        return (1 - high_half) * down + high_half * up

    def row_to(d):
        return (row + d) % n_row

    def row_from(d):
        return (row + n_row - d) % n_row

    local = [
        pltpu.make_async_copy(source, place, in_sem.at[i])
        for i, (source, place) in enumerate(
            [
                (primal_start, x_init.at[row, 0:sx]),
                (dual_start, y_init.at[col, 0:sy]),
                (rhs, y_init.at[col, sy : 2 * sy]),
                (cost, c_init.at[row, 0:sx]),
                (lower, c_init.at[row, sx : 2 * sx]),
                (upper, c_init.at[row, 2 * sx : 3 * sx]),
            ]
        )
    ]
    for copy in local:
        copy.start()
    part = slots // TILE_PARTS
    tile_copies = [
        pltpu.make_async_copy(
            tiles_hbm.at[i * part : (i + 1) * part], tiles.at[i * part : (i + 1) * part], tile_sem.at[i]
        )
        for i in range(TILE_PARTS)
    ]
    for copy in tile_copies:
        copy.start()

    mesh_id = pl.DeviceIdType.MESH
    barrier = pltpu.get_barrier_semaphore()
    for d in range(1, n_row):
        pl.semaphore_signal(barrier, inc=1, device_id={"row": row_to(d)}, device_id_type=mesh_id)
    for k in range(chips - 1):
        pl.semaphore_signal(
            barrier, inc=1, device_id={"col": chip_at(k) * 2 + core}, device_id_type=mesh_id
        )
    pl.semaphore_signal(barrier, inc=1, device_id={"col": partner}, device_id_type=mesh_id)

    live = lax.broadcasted_iota(jnp.int32, (1, slots), 1) < tile_count[...]
    for ids, init, me, at in ((tile_row, y_init, col, 2 * sy), (tile_col, x_init, row, sx)):
        init[me, at : at + SUB, :] = jnp.full((SUB, 128), -1.0, jnp.float32)
        init[me, at : at + SUB, 0:slots] = jnp.broadcast_to(
            jnp.where(live, ids[...].astype(jnp.float32), -1.0), (SUB, slots)
        )

    def remote(place, send, recv, target):
        return pltpu.make_async_remote_copy(
            src_ref=place, dst_ref=place, send_sem=send, recv_sem=recv, device_id=target, device_id_type=mesh_id
        )

    def row_send(place_of, send, recv, c):
        for d in range(1, n_row):
            remote(place_of(row, c), send(d - 1, c), recv(d - 1, c), {"row": row_to(d)}).start()

    def row_wait(place_of, send, recv, chunks):
        for c in range(chunks):
            for d in range(1, n_row):
                remote(place_of(row_from(d), c), send(d - 1, c), recv(d - 1, c), {"row": row_to(d)}).wait_recv()
        for c in range(chunks):
            for d in range(1, n_row):
                remote(place_of(row, c), send(d - 1, c), recv(d - 1, c), {"row": row_to(d)}).wait_send()

    def col_send(place_of, send, recv, c):
        for k in range(chips - 1):
            there = chip_at(k)
            remote(place_of(col, c), send(there, c), recv(chip, c), {"col": there * 2 + core}).start()
        remote(place_of(col, c), send(chip, c), recv(chip, c), {"col": partner}).start()

    def col_wait(place_of, send, recv, chunks):
        order = [(c, k) for c in range(chunks) for k in reversed(range(chips - 1))]
        to_partner = {"col": partner}
        for c, k in order:
            there = chip_at(k)
            block = place_of(there * 2 + core, c)
            remote(block, send(there, c), recv(there, c), to_partner).wait_recv()
            remote(block, send(chips + there, c), recv(chips + there, c), to_partner).start()
        for c in range(chunks):
            remote(place_of(partner, c), send(chip, c), recv(chip, c), to_partner).wait_recv()
        for c, k in order:
            there = chip_at(k)
            block = place_of(there * 2 + 1 - core, c)
            remote(block, send(chips + there, c), recv(chips + there, c), to_partner).wait_recv()
        for c, k in order:
            there = chip_at(k)
            remote(place_of(col, c), send(there, c), recv(chip, c), to_partner).wait_send()
            block = place_of(there * 2 + core, c)
            remote(block, send(chips + there, c), recv(chips + there, c), to_partner).wait_send()
        for c in range(chunks):
            remote(place_of(col, c), send(chip, c), recv(chip, c), to_partner).wait_send()

    def whole(buffer, send, recv):
        return (lambda i, c: buffer.at[i], lambda k, c: send.at[k], lambda k, c: recv.at[k])

    def sliced(buffer, send, recv, now):
        size = slots // CHUNKS
        return (
            lambda i, c: buffer.at[now, i, c * size : (c + 1) * size],
            lambda k, c: send.at[now, k, c],
            lambda k, c: recv.at[now, k, c],
        )

    xi = whole(x_init, xi_send, xi_recv)
    ci = whole(c_init, ci_send, ci_recv)
    yi = whole(y_init, yi_send, yi_recv)
    local[0].wait()
    pl.semaphore_wait(barrier, (n_row - 1) + (chips - 1) + 1)
    row_send(*xi, 0)
    for copy in local[1:3]:
        copy.wait()
    col_send(*yi, 0)
    for copy in local[3:]:
        copy.wait()
    row_send(*ci, 0)

    def pair_up(q, carry):
        for half in range(2):
            tile = tiles[2 * q + half]
            for out, data in ((plain, tile), (flipped, tile.T)):
                high = data.astype(jnp.bfloat16)
                out[q, 0:128, half * 128 : half * 128 + 128] = high
                out[q, 128:256, half * 128 : half * 128 + 128] = (
                    data - high.astype(jnp.float32)
                ).astype(jnp.bfloat16)
        return carry

    for i in range(TILE_PARTS):
        tile_copies[i].wait()
        lax.fori_loop(i * part // 2, (i + 1) * part // 2, pair_up, 0, unroll=2)

    def column_of(init, i, at):
        return init[i, at : at + SUB, :].T[:slots, 0:1]

    def own_ids(init, me, at):
        ids = column_of(init, me, at)
        return jnp.where(ids < 0.0, -2.0, ids)

    def hot_of(ids, first, share, column, hot, init, at, n):
        for i in range(n):
            column[i * slots : (i + 1) * slots, :] = jnp.broadcast_to(column_of(init, i, at), (slots, 128))
        wide = column[...].T[0:1, :]
        own = first + lax.broadcasted_iota(jnp.int32, (share, 1), 0)
        hot[0:slots, :] = jnp.where(ids == wide, 1.0, 0.0).astype(jnp.bfloat16)
        hot[slots : slots + share, :] = jnp.where(own.astype(jnp.float32) == wide, 1.0, 0.0).astype(jnp.bfloat16)

    def pick_of(ids, blocks):
        lanes = lax.broadcasted_iota(jnp.int32, (slots, blocks), 1).astype(jnp.float32)
        return jnp.where(ids == lanes, 1.0, 0.0).astype(jnp.bfloat16)

    def place_state(state, pick, init, at, share, me, n):
        state[0:slots, :] = split_dot(pick, init[:, at : at + share, :].reshape(n * share, 128))
        state[slots : slots + share, :] = init[me, at : at + share, :]

    def products(pairs, vectors, out, send):
        line = lax.broadcasted_iota(jnp.int32, (SUB, 128), 0)
        per_chunk = slots // SUB // CHUNKS

        def group(g, carry):
            at = pl.multiple_of(g * SUB, SUB)
            left = jnp.concatenate(pieces_of(vectors[pl.ds(at, SUB), :]), axis=0).astype(jnp.bfloat16)
            left = jnp.concatenate([left, left], axis=1)
            result = jnp.zeros((SUB, 128), jnp.float32)
            for q in range(SUB // 2):
                both = jnp.dot(left, pairs[g * (SUB // 2) + q], preferred_element_type=jnp.float32)
                total = (both[2 * SUB :] + both[SUB : 2 * SUB]) + both[:SUB]
                result = jnp.where(line == 2 * q, total[:, :128], result)
                result = jnp.where(line == 2 * q + 1, total[:, 128:], result)
            out[pl.ds(at, SUB), :] = result
            return carry

        for c in range(CHUNKS):
            lax.fori_loop(c * per_chunk, (c + 1) * per_chunk, group, 0, unroll=UNROLL)
            send(c)

    def forward(now):
        z = sliced(z_all, z_send, z_recv, now)
        products(flipped, extrapolated, z_all.at[now, col], lambda c: col_send(*z, c))

    row_wait(*xi, 1)
    col_ids = own_ids(x_init, row, sx)
    x_pick = pick_of(col_ids, n_row * sx)
    place_state(x_state, x_pick, x_init, 0, sx, row, n_row)
    extrapolated[...] = x_state[0:slots, :]
    forward(0)

    hot_of(col_ids, row * sx, sx, x_column, x_hot, x_init, sx, n_row)
    row_wait(*ci, 1)
    place_state(c_state, x_pick, c_init, 0, sx, row, n_row)
    place_state(l_state, x_pick, c_init, sx, sx, row, n_row)
    place_state(u_state, x_pick, c_init, 2 * sx, sx, row, n_row)
    col_wait(*yi, 1)
    row_ids = own_ids(y_init, col, 2 * sy)
    y_pick = pick_of(row_ids, n_col * sy)
    place_state(y_state, y_pick, y_init, 0, sy, col, n_col)
    place_state(b_state, y_pick, y_init, sy, sy, col, n_col)
    hot_of(row_ids, col * sy, sy, y_column, y_hot, y_init, 2 * sy, n_col)
    y_total[...] = jnp.zeros_like(y_total)
    x_total[...] = jnp.zeros_like(x_total)

    def iteration(step, carry):
        now = step % 2
        z = sliced(z_all, z_send, z_recv, now)
        p = sliced(p_all, p_send, p_recv, now)
        col_wait(*z, CHUNKS)
        applied = split_dot(y_hot[...], z_all[now].reshape(n_col * slots, 128))
        y_new = jnp.maximum(y_state[...] + dual_step * (b_state[...] - applied), 0.0)
        y_state[...] = y_new
        products(plain, y_state, p_all.at[now, row], lambda c: row_send(*p, c))
        y_total[...] += y_new[slots:, :]
        row_wait(*p, CHUNKS)
        transposed = split_dot(x_hot[...], p_all[now].reshape(n_row * slots, 128))
        x_old = x_state[...]
        moved = x_old - primal_step * (c_state[...] - transposed)
        x_new = jnp.minimum(jnp.maximum(moved, l_state[...]), u_state[...])
        x_state[...] = x_new
        extrapolated[...] = 2.0 * x_new[:slots, :] - x_old[:slots, :]

        @pl.when(step < ITERS - 1)
        def _():
            forward(1 - now)

        x_total[...] += x_new[slots:, :]
        return carry

    lax.fori_loop(0, ITERS, iteration, 0)

    primal_last[...] = x_state[slots:, :]
    dual_last[...] = y_state[slots:, :]
    primal_mean[...] = x_total[...] / ITERS
    dual_mean[...] = y_total[...] / ITERS


def body(n_row, n_col, tiles, tile_row, tile_col, tile_count, cost, rhs, lower, upper, primal_start, dual_start):
    slots, bs = tiles.shape[0], tiles.shape[2]
    blocks = [a.reshape(-1, bs) for a in (cost, rhs, lower, upper, primal_start, dual_start)]
    sx, sy = blocks[0].shape[0], blocks[1].shape[0]
    f32 = jnp.float32
    chips = n_col // 2
    vmem = pl.BlockSpec(memory_space=pltpu.VMEM)
    hbm = pl.BlockSpec(memory_space=pltpu.HBM)
    dma = pltpu.SemaphoreType.DMA
    state = lambda share: pltpu.VMEM((slots + share, bs), f32)
    out = pl.pallas_call(
        functools.partial(kernel, n_row, n_col),
        out_shape=[jax.ShapeDtypeStruct((s, bs), f32) for s in (sx, sy, sx, sy)],
        in_specs=[hbm] + [vmem] * 3 + [hbm] * 6,
        out_specs=[vmem] * 4,
        scratch_shapes=[
            pltpu.VMEM(tiles.shape, f32),
            pltpu.VMEM((slots // 2, 2 * bs, 2 * bs), jnp.bfloat16),
            pltpu.VMEM((slots // 2, 2 * bs, 2 * bs), jnp.bfloat16),
            pltpu.VMEM((n_col, 2 * sy + SUB, bs), f32),
            pltpu.VMEM((n_row, sx + SUB, bs), f32),
            pltpu.VMEM((n_row, 3 * sx, bs), f32),
            pltpu.VMEM((2, n_col, slots, bs), f32),
            pltpu.VMEM((2, n_row, slots, bs), f32),
            pltpu.VMEM((slots + sy, n_col * slots), jnp.bfloat16),
            pltpu.VMEM((slots + sx, n_row * slots), jnp.bfloat16),
            pltpu.VMEM((n_col * slots, bs), f32),
            pltpu.VMEM((n_row * slots, bs), f32),
            state(sy), state(sy), state(sx), state(sx), state(sx), state(sx),
            pltpu.VMEM((slots, bs), f32),
            pltpu.VMEM((sy, bs), f32),
            pltpu.VMEM((sx, bs), f32),
            dma((TILE_PARTS,)), dma((6,)),
            dma((2, 2 * chips, CHUNKS)), dma((2, 2 * chips, CHUNKS)),
            dma((2, n_row, CHUNKS)), dma((2, n_row, CHUNKS)),
            dma((2 * chips,)), dma((2 * chips,)),
            dma((n_row,)), dma((n_row,)),
            dma((n_row,)), dma((n_row,)),
        ],
        compiler_params=pltpu.CompilerParams(
            collective_id=0, has_side_effects=True, vmem_limit_bytes=40 * 1024 * 1024
        ),
        name="pdhg",
    )(tiles, tile_row.reshape(1, slots), tile_col.reshape(1, slots), tile_count, *blocks)
    return tuple(a.reshape(1, -1) for a in out)


def solution(mesh):
    return jax.shard_map(
        functools.partial(body, mesh.shape["row"], mesh.shape["col"]),
        mesh=mesh,
        in_specs=(
            P("row", "col", None),
            P("row", "col"),
            P("row", "col"),
            P("row", "col"),
            P("col", "row"),
            P("row", "col"),
            P("col", "row"),
            P("col", "row"),
            P("col", "row"),
            P("row", "col"),
        ),
        out_specs=(P("col", "row"), P("row", "col"), P("col", "row"), P("row", "col")),
        check_vma=False,
    )
```

time: 132 us -> 106 us (0.80)
  Pallas kernels: 119 us -> 92.5 us
    pallas_call x1, Pallas kernels: 119 us -> 92.5 us  [body(): pl.pallas_call(functools.partial(kernel, n_row, n_col), out_shape=[jax.Sh...]
    unnamed x20 -> x22, local copies, waits for them, and re-layouts: 11.3 us -> 11.1 us
where the time goes in v2:
time: 106 us; the launch traced here: 105 us
  Pallas kernels  92.5 us (87%)
  local copies, waits for them, and re-layouts  11.1 us (10%)
  between operations  1.31 us (1%)
    pallas_call x1, Pallas kernels, body(): pl.pallas_call(functools.partial(kernel, n_row, n_col), out_shape=[jax.Sh...  92.5 us
    unnamed x22, local copies, waits for them, and re-layouts  11.1 us

profile of v2, /device:TPU:0, one launch (start us, length us, event | category | flops | bytes accessed | tf_op | source)
XLA Modules:
  0.0 104.9 jit_solution(6355352990651934664)
XLA Ops:
  1.3 0.0 copy-start
  1.3 2.8 %copy-done = f32[96,128,128]{2,1,0:T(8,128)S(1)} copy-done((f32[96,128,128]{2,1,0:T(8,128)S(1)}, f32[96,128,128]{2,1,0:T(8,128)}, u32[]{:S(2)}) %copy-start) | copy-done | bytes 6291480
  4.1 0.0 copy-start.1
  4.1 0.8 copy-done.1
  4.8 0.0 copy-start.2
  4.8 0.8 copy-done.2
  5.6 0.0 copy-start.3
  5.6 0.8 copy-done.3
  6.3 0.0 copy-start.4
  6.3 0.8 copy-done.4
  7.1 0.0 copy-start.5
  7.1 0.8 copy-done.5
  7.9 0.0 copy-start.6
  7.9 0.8 copy-done.6
  8.6 0.0 copy-start.7
  8.6 0.7 copy-done.7
  9.3 0.0 copy-start.8
  9.3 0.7 copy-done.8
  9.9 92.5 %pdhg.1 = (f32[64,128]{1,0:T(8,128)S(1)}, f32[64,128]{1,0:T(8,128)S(1)}, f32[64,128]{1,0:T(8,128)S(1)}, f32[64,128]{1,0:T(8,128)S(1)}) custom-call(f32[96,128,128]{2,1,0:T(8,128)S(1)} %copy-done, s32[1,96]{1,0:T(1,128)S(1)} %bitcast.22, s32[1,96]{1,0:T(1,128)S(1)} %bitcast.23, s32[1,1]{1,0:T(1,128)S(6)} %copy.18.tile_count, f32[64,128]{1,0:T(8,128)S(1)} %bitcast.12, ...), custom_call_target="tpu_custom_call" | custom-call | tf_op jit(solution)/shard_map/pdhg/pallas_call | solution.py:304
  102.5 0.6 copy.19
  103.1 0.6 copy.20
  103.7 0.6 copy.21
  104.3 0.6 copy.22
Async XLA Ops:
  1.3 2.8 %copy-start = (f32[96,128,128]{2,1,0:T(8,128)S(1)}, f32[96,128,128]{2,1,0:T(8,128)}, u32[]{:S(2)}) copy-start(f32[96,128,128]{2,1,0:T(8,128)} %tiles_hbm.1) | copy-start | bytes 18874372
  4.1 0.8 copy-start.1
  4.8 0.8 copy-start.2
  5.6 0.8 copy-start.3
  6.3 0.8 copy-start.4
  7.1 0.8 copy-start.5
  7.9 0.8 copy-start.6
  8.6 0.7 copy-start.7
  9.3 0.7 copy-start.8

commit v3 on v2

--- a/solution.py
+++ b/solution.py
@@ -11,9 +11,10 @@
 primal_step = 0.3
 dual_step = 0.3
 SUB = 8
-CHUNKS = 2
+CHUNKS = 3
 TILE_PARTS = 4
-UNROLL = 6
+UNROLL = 4
+VMEM_BYTES = 62 * 1024 * 1024
 
 
 def split_dot(hot, data):
@@ -38,7 +39,7 @@
     primal_mean, dual_mean, primal_last, dual_last,
     tiles, plain, flipped, y_init, x_init, c_init, z_all, p_all, y_hot, x_hot, y_column, x_column,
     y_state, b_state, x_state, c_state, l_state, u_state, extrapolated, y_total, x_total,
-    tile_sem, in_sem, z_send, z_recv, p_send, p_recv, yi_send, yi_recv, xi_send, xi_recv, ci_send, ci_recv,
+    row_line, col_line, count_cell, tile_sem, in_sem, z_send, z_recv, p_send, p_recv, yi_send, yi_recv, xi_send, xi_recv, ci_send, ci_recv,
 ):
     slots = tile_row.shape[1]
     sy = rhs.shape[0]
@@ -73,6 +74,9 @@
                 (cost, c_init.at[row, 0:sx]),
                 (lower, c_init.at[row, sx : 2 * sx]),
                 (upper, c_init.at[row, 2 * sx : 3 * sx]),
+                (tile_row, row_line),
+                (tile_col, col_line),
+                (tile_count, count_cell),
             ]
         )
     ]
@@ -98,8 +102,10 @@
         )
     pl.semaphore_signal(barrier, inc=1, device_id={"col": partner}, device_id_type=mesh_id)
 
-    live = lax.broadcasted_iota(jnp.int32, (1, slots), 1) < tile_count[...]
-    for ids, init, me, at in ((tile_row, y_init, col, 2 * sy), (tile_col, x_init, row, sx)):
+    for copy in local[6:]:
+        copy.wait()
+    live = lax.broadcasted_iota(jnp.int32, (1, slots), 1) < count_cell[...]
+    for ids, init, me, at in ((row_line, y_init, col, 2 * sy), (col_line, x_init, row, sx)):
         init[me, at : at + SUB, :] = jnp.full((SUB, 128), -1.0, jnp.float32)
         init[me, at : at + SUB, 0:slots] = jnp.broadcast_to(
             jnp.where(live, ids[...].astype(jnp.float32), -1.0), (SUB, slots)
@@ -170,7 +176,7 @@
     for copy in local[1:3]:
         copy.wait()
     col_send(*yi, 0)
-    for copy in local[3:]:
+    for copy in local[3:6]:
         copy.wait()
     row_send(*ci, 0)
 
@@ -304,7 +310,7 @@
     out = pl.pallas_call(
         functools.partial(kernel, n_row, n_col),
         out_shape=[jax.ShapeDtypeStruct((s, bs), f32) for s in (sx, sy, sx, sy)],
-        in_specs=[hbm] + [vmem] * 3 + [hbm] * 6,
+        in_specs=[hbm] * 10,
         out_specs=[vmem] * 4,
         scratch_shapes=[
             pltpu.VMEM(tiles.shape, f32),
@@ -323,7 +329,8 @@
             pltpu.VMEM((slots, bs), f32),
             pltpu.VMEM((sy, bs), f32),
             pltpu.VMEM((sx, bs), f32),
-            dma((TILE_PARTS,)), dma((6,)),
+            pltpu.VMEM((1, slots), jnp.int32), pltpu.VMEM((1, slots), jnp.int32), pltpu.VMEM((1, 1), jnp.int32),
+            dma((TILE_PARTS,)), dma((9,)),
             dma((2, 2 * chips, CHUNKS)), dma((2, 2 * chips, CHUNKS)),
             dma((2, n_row, CHUNKS)), dma((2, n_row, CHUNKS)),
             dma((2 * chips,)), dma((2 * chips,)),
@@ -331,7 +338,7 @@
             dma((n_row,)), dma((n_row,)),
         ],
         compiler_params=pltpu.CompilerParams(
-            collective_id=0, has_side_effects=True, vmem_limit_bytes=40 * 1024 * 1024
+            collective_id=0, has_side_effects=True, vmem_limit_bytes=VMEM_BYTES
         ),
         name="pdhg",
     )(tiles, tile_row.reshape(1, slots), tile_col.reshape(1, slots), tile_count, *blocks)

time: 106 us -> 99.1 us (0.935)
  local copies, waits for them, and re-layouts: 11.1 us -> 5.5 us
    unnamed x22 -> x4, local copies, waits for them, and re-layouts: 11.1 us -> 5.5 us
where the time goes in v3:
time: 99.1 us; the launch traced here: 98.8 us
  Pallas kernels  92 us (93%)
  local copies, waits for them, and re-layouts  5.5 us (6%)
  between operations  1.29 us (1%)
    pallas_call x1, Pallas kernels, body(): pl.pallas_call(functools.partial(kernel, n_row, n_col), out_shape=[jax.Sh...  92 us
    unnamed x4, local copies, waits for them, and re-layouts  5.5 us

profile of v3, /device:TPU:0, one launch (start us, length us, event | category | flops | bytes accessed | tf_op | source)
XLA Modules:
  0.0 98.8 jit_solution(6576600605439256796)
XLA Ops:
  1.3 92.0 %pdhg.1 = (f32[64,128]{1,0:T(8,128)}, f32[64,128]{1,0:T(8,128)}, f32[64,128]{1,0:T(8,128)}, f32[64,128]{1,0:T(8,128)}) custom-call(f32[96,128,128]{2,1,0:T(8,128)} %tiles_hbm.1, s32[1,96]{1,0:T(1,128)} %bitcast.22, s32[1,96]{1,0:T(1,128)} %bitcast.23, s32[1,1]{1,0:T(1,128)S(6)} %copy.18.tile_count, f32[64,128]{1,0:T(8,128)} %bitcast.12, f32[64,128]{1,0:T(8,128)} %bitcast.13, ...), custom_call_target="tpu_custom_call" | custom-call | tf_op jit(solution)/shard_map/pdhg/pallas_call | solution.py:310
  93.3 1.4 %copy.19 = f32[1,8192]{1,0:T(1,128)} copy(f32[1,8192]{1,0:T(1,128)} %bitcast.21) | data formatting | bytes 65536
  94.6 1.4 %copy.20 = f32[1,8192]{1,0:T(1,128)} copy(f32[1,8192]{1,0:T(1,128)} %bitcast.20) | data formatting | bytes 65536
  96.0 1.4 %copy.21 = f32[1,8192]{1,0:T(1,128)} copy(f32[1,8192]{1,0:T(1,128)} %bitcast.19) | data formatting | bytes 65536
  97.4 1.4 %copy.22 = f32[1,8192]{1,0:T(1,128)} copy(f32[1,8192]{1,0:T(1,128)} %bitcast.18) | data formatting | bytes 65536
